TPU v7x, 32 devices: a whole 2x2x4 slice. The times are simulated.
32 devices in a mesh: rows: 8 (over y, x, core), blk: 4 (over z).
Axes of the slice: x: 2, y: 2, z: 4, core: 2. Of those that a mesh axis runs over, the one named last changes fastest.
Arguments:
- vectors: float32 [6144, 128], P('blk'), may hold values from -6 to 6
- left_intersection: float32 [256, 128, 128], P(('rows', 'blk')), may hold values from -0.5 to 0.5
- right_intersection: float32 [48, 128, 128], P('blk'), may hold values from -0.5 to 0.5
- tiles: float32 [512, 128, 128], P('rows'), may hold values from -0.09375 to 0.09375
- pair_cols: int32 [256, 32], P(('rows', 'blk')), may hold values from 0 to 47, all different within a row
- pair_owner: int32 [256, 32], P(('rows', 'blk')), may hold values from 0 to 7, as said below
- pair_slot: int32 [256, 32], P(('rows', 'blk')), may hold values from 0 to 63
- pair_counts: int32 [256], P(('rows', 'blk')), may hold values from 1 to 32, as said below
Outputs:
- product: float32 [32768, 128], P(('rows', 'blk'))
Inputs may be any that keep to these rules, and one draw needn't show every extreme that they name: `pair_owner`: among the 256 entries of each aligned block of 8 row blocks, every rows index appears exactly 32 times. `pair_cols`: the column blocks listed for one row block are distinct. `pair_counts`: some row block has all 32 entries live.
All inputs are finite; a program needn't handle non-finite values.
Results may differ from a plain program's by a relative error of at most 0.0003.
Values sent between devices are 32-bit elements; how exact they have to be, the bound alone decides.
No kernel may reach another device: no remote copies, remote signals or barrier semaphores. Data moves between devices by JAX's collectives and lax.ppermute only.
A program may use at most 128 MiB of HBM per device.

v0:
```python
import jax
import jax.numpy as jnp
from jax import lax
from jax.sharding import PartitionSpec as P


def pick_rows(table, row_ids, table_rows):
    onehot = (row_ids[:, None] == jnp.arange(table_rows)[None, :]).astype(jnp.float32)
    flat = table.reshape(table_rows, -1)
    picked = jnp.dot(
        onehot, flat, precision=lax.Precision.HIGHEST, preferred_element_type=jnp.float32
    )
    return picked.reshape((row_ids.shape[0],) + table.shape[1:])


def invert_slots(values, slot_index):
    count = slot_index.shape[0]
    matches = slot_index[None, :] == jnp.arange(count)[:, None]
    return jnp.sum(jnp.where(matches, values[None, :], 0), axis=1)


def per_device(
    vectors,
    left_intersection,
    right_intersection,
    tiles,
    pair_cols,
    pair_owner,
    pair_slot,
    pair_counts,
):
    row_blocks, fine_rows, coarse = left_intersection.shape
    listed = pair_cols.shape[1]
    vec_count = vectors.shape[1]
    owners = lax.axis_size("rows")
    entries = row_blocks * listed
    per_owner = entries // owners
    highest = lax.Precision.HIGHEST
    held_tiles = tiles.shape[0]
    flat_owner = pair_owner.reshape(entries)
    earlier = jnp.arange(entries)[:, None] > jnp.arange(entries)[None, :]
    matches = flat_owner[:, None] == flat_owner[None, :]
    position = jnp.sum(jnp.where(matches & earlier, 1, 0), axis=1).astype(jnp.int32)
    slot_index = flat_owner * per_owner + position
    local_blocks = vectors.reshape(right_intersection.shape[0], fine_rows, vec_count)
    entry_ids = jnp.arange(entries)
    block_ids = entry_ids // listed
    count_each = jnp.repeat(pair_counts, listed)
    live_flags = (entry_ids % listed < count_each).astype(jnp.int32)
    block_range = jnp.arange(row_blocks)
    slot_req = invert_slots(pair_slot.reshape(entries), slot_index)
    col_req = invert_slots(pair_cols.reshape(entries), slot_index)
    block_req = invert_slots(block_ids, slot_index)
    live_req = invert_slots(live_flags, slot_index)
    stacked = jnp.stack([slot_req, col_req, block_req, live_req]).reshape(4, owners, per_owner)
    received = lax.all_to_all(stacked, "rows", split_axis=1, concat_axis=1, tiled=True)
    local_proj = jnp.einsum("csu,csv->cuv", right_intersection, local_blocks, precision=highest)
    proj_all = lax.all_gather(local_proj, "blk", axis=0, tiled=True)
    col_total = proj_all.shape[0]

    def per_source(packed):
        slots_here, cols_here, blocks_here, live_here = packed
        chosen = pick_rows(tiles, slots_here, held_tiles)
        picked = pick_rows(proj_all, cols_here, col_total)
        applied = jnp.einsum("ptu,puv->ptv", chosen, picked, precision=highest)
        weights = (
            (blocks_here[None, :] == block_range[:, None]) & (live_here[None, :] > 0)
        ).astype(jnp.float32)
        return jnp.einsum("rp,ptv->rtv", weights, applied, precision=highest)

    partial_sums = lax.map(per_source, (received[0], received[1], received[2], received[3]))
    returned = lax.all_to_all(partial_sums, "rows", split_axis=0, concat_axis=0, tiled=True)
    summed = jnp.sum(returned, axis=0)
    result = jnp.einsum("bft,btv->bfv", left_intersection, summed, precision=highest)
    return result.reshape(row_blocks * fine_rows, vec_count)


def solution(mesh):
    return jax.shard_map(
        per_device,
        mesh=mesh,
        in_specs=(
            P("blk", None),
            P(("rows", "blk"), None, None),
            P("blk", None, None),
            P("rows", None, None),
            P(("rows", "blk"), None),
            P(("rows", "blk"), None),
            P(("rows", "blk"), None),
            P(("rows", "blk")),
        ),
        out_specs=P(("rows", "blk"), None),
        check_vma=False,
    )
```

profile of v0, /device:TPU:0, one launch (start us, length us, event | category | flops | bytes accessed | tf_op | source)
XLA Modules:
  0.0 277.5 jit_solution(6628994686971753800)
XLA Ops:
  7.7 3.4 %fusion.40 = f32[12,128,128]{2,1,0:T(8,128)} fusion(f32[12,128,128]{2,1,0:T(8,128)} %param.12, f32[12,128,128]{2,1,0:T(8,128)S(1)} %bitcast.91), kind=kOutput, calls=%fused_computation.57 | convolution fusion | flops 301989888 | bytes 2359296 | tf_op jit(solution)/shard_map/csu,csv->cuv/dot_general | solution.py:57
  13.0 5.2 %all-to-all-start = ((s32[8,1,128]{2,1,0:T(1,128)}), s32[8,1,128]{2,1,0:T(1,128)S(1)}, u32[]{:S(2)}, u32[]{:S(2)}) async-start(s32[8,1,128]{2,1,0:T(1,128)} %reshape.85), calls=%async_computation | async-start | bytes 8192 | tf_op jit(solution)/shard_map/all_to_all | solution.py:56
  18.2 4.6 %all-to-all-done = s32[8,1,128]{2,1,0:T(1,128)S(1)} async-done(((s32[8,1,128]{2,1,0:T(1,128)}), s32[8,1,128]{2,1,0:T(1,128)S(1)}, u32[]{:S(2)}, u32[]{:S(2)}) %all-to-all-start) | async-done | bytes 4128 | tf_op jit(solution)/shard_map/all_to_all | solution.py:56
  24.1 53.3 %all-gather.2.cloned.1.call-done = f32[48,128,128]{2,1,0:T(8,128)} async-done(((f32[12,128,128]{2,1,0:T(8,128)}), f32[48,128,128]{2,1,0:T(8,128)}) %all-gather.2.cloned.1.call-update) | async-done | bytes 3145744 | tf_op jit(solution)/shard_map/all_gather | solution.py:58
  77.5 135.7 %while.11 = (s32[]{:T(128)}, f32[8,8,128,128]{3,1,2,0:T(8,128)}, s32[8,32]{1,0:T(8,128)S(1)}, s32[8,32]{1,0:T(8,128)S(1)}, s32[8,32]{1,0:T(8,128)S(1)}, /*index=...) while((s32[]{:T(128)}, f32[8,8,128,128]{3,1,2,0:T(8,128)}, ...), condition=%wide.region_6.7_spmd.clone, body=%wide.region_5.6_spmd.clone.sunk | while | flops 1560285184 | bytes 33032132 | solution.py:71
  77.5 6.2 %fusion.69 = f32[32,128,128]{2,0,1:T(8,128)S(1)} fusion(s32[32]{0:T(128)S(1)} %get-tuple-element.150, f32[8,8,128,128]{3,2,1,0:T(8,128)} %bitcast.92), kind=kOutput, calls=%fused_computation.2.clone.1 | convolution fusion | flops 402655232 | bytes 6291584 | tf_op jit(solution)/shard_map/while/body/eval_jaxpr/dot_general | solution.py:10
  87.0 4.6 %fusion.70 = f32[32,128,128]{2,1,0:T(8,128)S(1)} fusion(f32[32,128,128]{2,0,1:T(8,128)S(1)} %fusion.67, f32[32,128,128]{2,0,1:T(8,128)S(1)} %fusion.69), kind=kOutput, calls=%fused_computation.11.clone.1 | convolution fusion | flops 805306368 | bytes 6291456 | tf_op jit(solution)/shard_map/while/body/eval_jaxpr/ptu,puv->ptv/dot_general | solution.py:65
  94.4 6.2 %fusion.69 = f32[32,128,128]{2,0,1:T(8,128)S(1)} fusion(s32[32]{0:T(128)S(1)} %get-tuple-element.150, f32[8,8,128,128]{3,2,1,0:T(8,128)} %bitcast.92), kind=kOutput, calls=%fused_computation.2.clone.1 | convolution fusion | flops 402655232 | bytes 6291584 | tf_op jit(solution)/shard_map/while/body/eval_jaxpr/dot_general | solution.py:10
  100.6 3.3 %fusion.67 = f32[32,128,128]{2,0,1:T(8,128)S(1)} fusion(s32[32]{0:T(128)S(1)} %fusion.66, f32[6,8,128,128]{3,2,1,0:T(8,128)S(1)} %bitcast.93), kind=kOutput, calls=%fused_computation.6.clone.1 | convolution fusion | flops 301991424 | bytes 5243008 | tf_op jit(solution)/shard_map/while/body/eval_jaxpr/dot_general | solution.py:10
  104.0 4.6 %fusion.70 = f32[32,128,128]{2,1,0:T(8,128)S(1)} fusion(f32[32,128,128]{2,0,1:T(8,128)S(1)} %fusion.67, f32[32,128,128]{2,0,1:T(8,128)S(1)} %fusion.69), kind=kOutput, calls=%fused_computation.11.clone.1 | convolution fusion | flops 805306368 | bytes 6291456 | tf_op jit(solution)/shard_map/while/body/eval_jaxpr/ptu,puv->ptv/dot_general | solution.py:65
  111.4 6.2 %fusion.69 = f32[32,128,128]{2,0,1:T(8,128)S(1)} fusion(s32[32]{0:T(128)S(1)} %get-tuple-element.150, f32[8,8,128,128]{3,2,1,0:T(8,128)} %bitcast.92), kind=kOutput, calls=%fused_computation.2.clone.1 | convolution fusion | flops 402655232 | bytes 6291584 | tf_op jit(solution)/shard_map/while/body/eval_jaxpr/dot_general | solution.py:10
  120.9 4.6 %fusion.70 = f32[32,128,128]{2,1,0:T(8,128)S(1)} fusion(f32[32,128,128]{2,0,1:T(8,128)S(1)} %fusion.67, f32[32,128,128]{2,0,1:T(8,128)S(1)} %fusion.69), kind=kOutput, calls=%fused_computation.11.clone.1 | convolution fusion | flops 805306368 | bytes 6291456 | tf_op jit(solution)/shard_map/while/body/eval_jaxpr/ptu,puv->ptv/dot_general | solution.py:65
  128.3 6.2 %fusion.69 = f32[32,128,128]{2,0,1:T(8,128)S(1)} fusion(s32[32]{0:T(128)S(1)} %get-tuple-element.150, f32[8,8,128,128]{3,2,1,0:T(8,128)} %bitcast.92), kind=kOutput, calls=%fused_computation.2.clone.1 | convolution fusion | flops 402655232 | bytes 6291584 | tf_op jit(solution)/shard_map/while/body/eval_jaxpr/dot_general | solution.py:10
  137.9 4.6 %fusion.70 = f32[32,128,128]{2,1,0:T(8,128)S(1)} fusion(f32[32,128,128]{2,0,1:T(8,128)S(1)} %fusion.67, f32[32,128,128]{2,0,1:T(8,128)S(1)} %fusion.69), kind=kOutput, calls=%fused_computation.11.clone.1 | convolution fusion | flops 805306368 | bytes 6291456 | tf_op jit(solution)/shard_map/while/body/eval_jaxpr/ptu,puv->ptv/dot_general | solution.py:65
  145.3 6.2 %fusion.69 = f32[32,128,128]{2,0,1:T(8,128)S(1)} fusion(s32[32]{0:T(128)S(1)} %get-tuple-element.150, f32[8,8,128,128]{3,2,1,0:T(8,128)} %bitcast.92), kind=kOutput, calls=%fused_computation.2.clone.1 | convolution fusion | flops 402655232 | bytes 6291584 | tf_op jit(solution)/shard_map/while/body/eval_jaxpr/dot_general | solution.py:10
  151.5 3.3 %fusion.67 = f32[32,128,128]{2,0,1:T(8,128)S(1)} fusion(s32[32]{0:T(128)S(1)} %fusion.66, f32[6,8,128,128]{3,2,1,0:T(8,128)S(1)} %bitcast.93), kind=kOutput, calls=%fused_computation.6.clone.1 | convolution fusion | flops 301991424 | bytes 5243008 | tf_op jit(solution)/shard_map/while/body/eval_jaxpr/dot_general | solution.py:10
  154.9 4.6 %fusion.70 = f32[32,128,128]{2,1,0:T(8,128)S(1)} fusion(f32[32,128,128]{2,0,1:T(8,128)S(1)} %fusion.67, f32[32,128,128]{2,0,1:T(8,128)S(1)} %fusion.69), kind=kOutput, calls=%fused_computation.11.clone.1 | convolution fusion | flops 805306368 | bytes 6291456 | tf_op jit(solution)/shard_map/while/body/eval_jaxpr/ptu,puv->ptv/dot_general | solution.py:65
  162.2 6.2 %fusion.69 = f32[32,128,128]{2,0,1:T(8,128)S(1)} fusion(s32[32]{0:T(128)S(1)} %get-tuple-element.150, f32[8,8,128,128]{3,2,1,0:T(8,128)} %bitcast.92), kind=kOutput, calls=%fused_computation.2.clone.1 | convolution fusion | flops 402655232 | bytes 6291584 | tf_op jit(solution)/shard_map/while/body/eval_jaxpr/dot_general | solution.py:10
  171.8 4.6 %fusion.70 = f32[32,128,128]{2,1,0:T(8,128)S(1)} fusion(f32[32,128,128]{2,0,1:T(8,128)S(1)} %fusion.67, f32[32,128,128]{2,0,1:T(8,128)S(1)} %fusion.69), kind=kOutput, calls=%fused_computation.11.clone.1 | convolution fusion | flops 805306368 | bytes 6291456 | tf_op jit(solution)/shard_map/while/body/eval_jaxpr/ptu,puv->ptv/dot_general | solution.py:65
  179.2 6.2 %fusion.69 = f32[32,128,128]{2,0,1:T(8,128)S(1)} fusion(s32[32]{0:T(128)S(1)} %get-tuple-element.150, f32[8,8,128,128]{3,2,1,0:T(8,128)} %bitcast.92), kind=kOutput, calls=%fused_computation.2.clone.1 | convolution fusion | flops 402655232 | bytes 6291584 | tf_op jit(solution)/shard_map/while/body/eval_jaxpr/dot_general | solution.py:10
  188.8 4.6 %fusion.70 = f32[32,128,128]{2,1,0:T(8,128)S(1)} fusion(f32[32,128,128]{2,0,1:T(8,128)S(1)} %fusion.67, f32[32,128,128]{2,0,1:T(8,128)S(1)} %fusion.69), kind=kOutput, calls=%fused_computation.11.clone.1 | convolution fusion | flops 805306368 | bytes 6291456 | tf_op jit(solution)/shard_map/while/body/eval_jaxpr/ptu,puv->ptv/dot_general | solution.py:65
  196.1 6.2 %fusion.69 = f32[32,128,128]{2,0,1:T(8,128)S(1)} fusion(s32[32]{0:T(128)S(1)} %get-tuple-element.150, f32[8,8,128,128]{3,2,1,0:T(8,128)} %bitcast.92), kind=kOutput, calls=%fused_computation.2.clone.1 | convolution fusion | flops 402655232 | bytes 6291584 | tf_op jit(solution)/shard_map/while/body/eval_jaxpr/dot_general | solution.py:10
  205.7 4.6 %fusion.70 = f32[32,128,128]{2,1,0:T(8,128)S(1)} fusion(f32[32,128,128]{2,0,1:T(8,128)S(1)} %fusion.67, f32[32,128,128]{2,0,1:T(8,128)S(1)} %fusion.69), kind=kOutput, calls=%fused_computation.11.clone.1 | convolution fusion | flops 805306368 | bytes 6291456 | tf_op jit(solution)/shard_map/while/body/eval_jaxpr/ptu,puv->ptv/dot_general | solution.py:65
  213.1 53.5 %all_to_all.10 = f32[8,8,128,128]{3,1,2,0:T(8,128)} all-to-all(f32[8,8,128,128]{3,1,2,0:T(8,128)} %get-tuple-element.52), channel_id=1, replica_groups=mesh['rows'=8,'blk'=4] {'rows'}, dimensions={0} | all-to-all | bytes 8388608 | tf_op jit(solution)/shard_map/all_to_all | solution.py:72
  (90 shorter events, 50.6 us)
Async XLA Ops:
  6.5 1.1 copy-start
  6.5 4.6 %copy-start.3 = (s32[8,32]{1,0:T(8,128)S(1)}, s32[8,32]{1,0:T(8,128)}, u32[]{:S(2)}) copy-start(s32[8,32]{1,0:T(8,128)} %param.15) | copy-start | bytes 3076
  6.5 4.7 %copy-start.6 = (s32[8]{0:T(128)S(1)}, s32[8]{0:T(128)}, u32[]{:S(2)}) copy-start(s32[8]{0:T(128)} %param.17) | copy-start | bytes 100
  6.5 4.8 %copy-start.4 = (s32[8,32]{1,0:T(8,128)S(1)}, s32[8,32]{1,0:T(8,128)}, u32[]{:S(2)}) copy-start(s32[8,32]{1,0:T(8,128)} %param.16) | copy-start | bytes 3076
  6.5 4.9 %copy-start.5 = (s32[8,32]{1,0:T(8,128)S(1)}, s32[8,32]{1,0:T(8,128)}, u32[]{:S(2)}) copy-start(s32[8,32]{1,0:T(8,128)} %param.14) | copy-start | bytes 3076
  6.5 70.9 %all-gather.2.cloned.1.call-start = ((), (), s32[]{:S(2)}) async-start(), calls=%async_computation.2 | async-start | bytes 3932160 | tf_op jit(solution)/shard_map/all_gather | solution.py:58
  13.0 9.8 %all-to-all-start = ((s32[8,1,128]{2,1,0:T(1,128)}), s32[8,1,128]{2,1,0:T(1,128)S(1)}, u32[]{:S(2)}, u32[]{:S(2)}) async-start(s32[8,1,128]{2,1,0:T(1,128)} %reshape.85), calls=%async_computation | async-start | bytes 8192 | tf_op jit(solution)/shard_map/all_to_all | solution.py:56
  77.5 6.2 %copy-start.1 = (f32[48,128,128]{2,1,0:T(8,128)S(1)}, f32[48,128,128]{2,1,0:T(8,128)}, u32[]{:S(2)}) copy-start(f32[48,128,128]{2,1,0:T(8,128)} %get-tuple-element.177) | copy-start | bytes 9437188 | tf_op jit(solution)/shard_map/while
  94.4 6.2 %copy-start.1 = (f32[48,128,128]{2,1,0:T(8,128)S(1)}, f32[48,128,128]{2,1,0:T(8,128)}, u32[]{:S(2)}) copy-start(f32[48,128,128]{2,1,0:T(8,128)} %get-tuple-element.177) | copy-start | bytes 9437188 | tf_op jit(solution)/shard_map/while
  111.4 6.2 %copy-start.1 = (f32[48,128,128]{2,1,0:T(8,128)S(1)}, f32[48,128,128]{2,1,0:T(8,128)}, u32[]{:S(2)}) copy-start(f32[48,128,128]{2,1,0:T(8,128)} %get-tuple-element.177) | copy-start | bytes 9437188 | tf_op jit(solution)/shard_map/while
  128.3 6.2 %copy-start.1 = (f32[48,128,128]{2,1,0:T(8,128)S(1)}, f32[48,128,128]{2,1,0:T(8,128)}, u32[]{:S(2)}) copy-start(f32[48,128,128]{2,1,0:T(8,128)} %get-tuple-element.177) | copy-start | bytes 9437188 | tf_op jit(solution)/shard_map/while
  145.3 6.2 %copy-start.1 = (f32[48,128,128]{2,1,0:T(8,128)S(1)}, f32[48,128,128]{2,1,0:T(8,128)}, u32[]{:S(2)}) copy-start(f32[48,128,128]{2,1,0:T(8,128)} %get-tuple-element.177) | copy-start | bytes 9437188 | tf_op jit(solution)/shard_map/while
  162.2 6.2 %copy-start.1 = (f32[48,128,128]{2,1,0:T(8,128)S(1)}, f32[48,128,128]{2,1,0:T(8,128)}, u32[]{:S(2)}) copy-start(f32[48,128,128]{2,1,0:T(8,128)} %get-tuple-element.177) | copy-start | bytes 9437188 | tf_op jit(solution)/shard_map/while
  179.2 6.2 %copy-start.1 = (f32[48,128,128]{2,1,0:T(8,128)S(1)}, f32[48,128,128]{2,1,0:T(8,128)}, u32[]{:S(2)}) copy-start(f32[48,128,128]{2,1,0:T(8,128)} %get-tuple-element.177) | copy-start | bytes 9437188 | tf_op jit(solution)/shard_map/while
  196.1 6.2 %copy-start.1 = (f32[48,128,128]{2,1,0:T(8,128)S(1)}, f32[48,128,128]{2,1,0:T(8,128)}, u32[]{:S(2)}) copy-start(f32[48,128,128]{2,1,0:T(8,128)} %get-tuple-element.177) | copy-start | bytes 9437188 | tf_op jit(solution)/shard_map/while
  266.6 2.5 copy-start.2
Sparse Core Ops, SparseCore 0:
  11.2 66.1 all-gather.1
where the time goes:
time: 278 us; the launch traced here: 277 us
  matrix products  140 us (50%)
  waiting for transfers between devices  58 us (21%)
  blocking collectives  53.5 us (19%)
  between operations  13.5 us (5%)
  starting transfers between devices  5.24 us (2%)
  other arithmetic  3.71 us (1%)
  local copies, waits for them, and re-layouts  3.25 us (1%)
    dot_general x16, matrix products, pick_rows(): jnp.dot(onehot, flat, precision=lax.Precision.HIGHEST, preferred_element_...  76.3 us
    all_to_all x1, blocking collectives, per_device(): lax.all_to_all(partial_sums, 'rows', split_axis=0, concat_axis=0, tiled=T...  53.5 us
    all_gather x1, waiting for transfers between devices, per_device(): proj_all = lax.all_gather(local_proj, 'blk', axis=0, tiled=True)  53.3 us
    dot_general x8, matrix products, per_source(): applied = jnp.einsum('ptu,puv->ptv', chosen, picked, precision=highest)  36.6 us
    dot_general x8, matrix products, per_source(): return jnp.einsum('rp,ptv->rtv', weights, applied, precision=highest)  22.2 us
  transfers between devices with their start and end apart: 2, of which 2 were waited for; matrix products, arithmetic and copies ran while one was open for 1% of the time, Pallas kernels for 0%

commit v1 on v0

--- a/solution.py
+++ b/solution.py
@@ -2,6 +2,24 @@
 import jax.numpy as jnp
 from jax import lax
 from jax.sharding import PartitionSpec as P
+
+
+def samples_all_advance(x_in, row_axis="blk"):
+    lower = lax.axis_size(row_axis)
+    f_now, now, y = (lower, lax.axis_index(row_axis), x_in.shape[0])
+    lanes = [(rr, (rr + 1) % f_now) for rr in range(f_now)]
+    s_next = jnp.zeros((*x_in.shape[:0], f_now * y, *x_in.shape[1:]), x_in.dtype)
+    s_next = lax.dynamic_update_slice_in_dim(s_next, x_in, now * y, axis=0)
+    copies = [(rr, (rr - 1) % f_now) for rr in range(f_now)]
+    block_next = f_now // 2
+    field_out = q_next = x_in
+    for kk in tuple(range(1, block_next + 1)):
+        field_out = lax.ppermute(field_out, axis_name=row_axis, perm=lanes)
+        s_next = lax.dynamic_update_slice_in_dim(s_next, field_out, (now - kk) % f_now * y, axis=0)
+        if kk < f_now - block_next:
+            q_next = lax.ppermute(q_next, perm=copies, axis_name=row_axis)
+            s_next = lax.dynamic_update_slice_in_dim(s_next, q_next, (now + kk) % f_now * y, axis=0)
+    return s_next
 
 
 def pick_rows(table, row_ids, table_rows):
@@ -55,7 +73,7 @@
     stacked = jnp.stack([slot_req, col_req, block_req, live_req]).reshape(4, owners, per_owner)
     received = lax.all_to_all(stacked, "rows", split_axis=1, concat_axis=1, tiled=True)
     local_proj = jnp.einsum("csu,csv->cuv", right_intersection, local_blocks, precision=highest)
-    proj_all = lax.all_gather(local_proj, "blk", axis=0, tiled=True)
+    proj_all = samples_all_advance(local_proj)
     col_total = proj_all.shape[0]
 
     def per_source(packed):

time: 278 us -> 269 us (0.968)
  waiting for transfers between devices: 58 us -> 42.5 us
  between operations: 13.5 us -> 0.07 us
  matrix products: 140 us -> 151 us
  local copies, waits for them, and re-layouts: 3.25 us -> 8.19 us
  starting transfers between devices: 5.24 us -> 9.03 us
    all_gather x1 -> x0, waiting for transfers between devices: 53.3 us -> none  [per_device(): proj_all = lax.all_gather(local_proj, 'blk', axis=0, tiled=True)]
    ppermute x0 -> x3, waiting for transfers between devices: none -> 37.8 us  [the longest x2 34.4 us: samples_all_advance(): field_out = lax.ppermute(field_out, axis_name=row_axis, perm=lanes)]
    dot_general x16, matrix products: 76.3 us -> 88.6 us  [pick_rows(): jnp.dot(onehot, flat, precision=lax.Precision.HIGHEST, preferred_element_...]
    ppermute x0 -> x3, starting transfers between devices: none -> 5.07 us  [the longest x2 3.06 us: samples_all_advance(): field_out = lax.ppermute(field_out, axis_name=row_axis, perm=lanes)]
    dynamic_update_slice x0 -> x3, local copies, waits for them, and re-layouts: none -> 2.85 us  [the longest x2 1.9 us: samples_all_advance(): lax.dynamic_update_slice_in_dim(s_next, field_out, (now - kk) % f_now * y...]
  transfers between devices with their start and end apart: 2 -> 4, of which waited for: 2 -> 4; matrix products, arithmetic and copies ran while one was open for 1% -> 2% of each run, Pallas kernels for 0% -> 0%
where the time goes in v1:
time: 269 us
  matrix products  151 us (56%)
  blocking collectives  53.5 us (20%)
  waiting for transfers between devices  42.5 us (16%)
  starting transfers between devices  9.03 us (3%)
  local copies, waits for them, and re-layouts  8.19 us (3%)
  other arithmetic  3.71 us (1%)
    dot_general x16, matrix products, pick_rows(): jnp.dot(onehot, flat, precision=lax.Precision.HIGHEST, preferred_element_...  88.6 us
    all_to_all x1, blocking collectives, per_device(): lax.all_to_all(partial_sums, 'rows', split_axis=0, concat_axis=0, tiled=T...  53.5 us
    dot_general x8, matrix products, per_source(): applied = jnp.einsum('ptu,puv->ptv', chosen, picked, precision=highest)  36.6 us
    ppermute x2, waiting for transfers between devices, samples_all_advance(): field_out = lax.ppermute(field_out, axis_name=row_axis, perm=lanes)  34.4 us
    dot_general x8, matrix products, per_source(): return jnp.einsum('rp,ptv->rtv', weights, applied, precision=highest)  22.2 us
  transfers between devices with their start and end apart: 4, of which 4 were waited for; matrix products, arithmetic and copies ran while one was open for 2% of the time, Pallas kernels for 0%

profile of v1, /device:TPU:0, one launch (start us, length us, event | category | flops | bytes accessed | tf_op | source)
XLA Modules:
  0.0 268.7 jit_solution(16089396058646462645)
XLA Ops:
  11.3 18.2 %collective-permute-done = f32[12,128,128]{2,1,0:T(8,128)S(1)} collective-permute-done((f32[12,128,128]{2,1,0:T(8,128)}, f32[12,128,128]{2,1,0:T(8,128)S(1)}, u32[]{:S(2)}, u32[]{:S(2)}) %collective-permute-start) | collective-permute-done | bytes 786464 | tf_op jit(solution)/shard_map/ppermute | solution.py:17
  34.9 4.6 %all-to-all-done = s32[8,1,128]{2,1,0:T(1,128)S(1)} async-done(((s32[8,1,128]{2,1,0:T(1,128)}), s32[8,1,128]{2,1,0:T(1,128)S(1)}, u32[]{:S(2)}, u32[]{:S(2)}) %all-to-all-start) | async-done | bytes 4128 | tf_op jit(solution)/shard_map/all_to_all | solution.py:74
  46.1 16.2 %collective-permute-done.2 = f32[12,128,128]{2,1,0:T(8,128)S(1)} collective-permute-done((f32[12,128,128]{2,1,0:T(8,128)S(1)}, f32[12,128,128]{2,1,0:T(8,128)S(1)}, u32[]{:S(2)}, u32[]{:S(2)}) %collective-permute-start.2) | collective-permute-done | bytes 786464 | tf_op jit(solution)/shard_map/ppermute | solution.py:17
  63.3 147.8 %while.11 = (s32[]{:T(128)}, f32[8,8,128,128]{3,1,2,0:T(8,128)}, s32[8,32]{1,0:T(8,128)S(1)}, s32[8,32]{1,0:T(8,128)S(1)}, s32[8,32]{1,0:T(8,128)S(1)}, /*index=...) while((s32[]{:T(128)}, f32[8,8,128,128]{3,1,2,0:T(8,128)}, ...), condition=%wide.region_6.7_spmd.clone, body=%wide.region_5.6_spmd.clone.sunk | while | flops 1560285184 | bytes 20449192 | solution.py:89
  63.3 6.1 %fusion.68 = f32[32,128,128]{2,0,1:T(8,128)S(1)} fusion(s32[32]{0:T(128)S(1)} %get-tuple-element.152, f32[8,8,128,128]{3,2,1,0:T(8,128)} %bitcast.92), kind=kOutput, calls=%fused_computation.2.clone.1 | convolution fusion | flops 402655232 | bytes 6291584 | tf_op jit(solution)/shard_map/while/body/eval_jaxpr/dot_general | solution.py:28
  69.4 5.0 %fusion.66 = f32[32,128,128]{2,0,1:T(8,128)S(1)} fusion(s32[32]{0:T(128)S(1)} %fusion.65, f32[6,8,128,128]{3,2,1,0:T(8,128)} %bitcast.89), kind=kOutput, calls=%fused_computation.6.clone.1 | convolution fusion | flops 301991424 | bytes 5243008 | tf_op jit(solution)/shard_map/while/body/eval_jaxpr/dot_general | solution.py:28
  74.4 4.6 %fusion.69 = f32[32,128,128]{2,1,0:T(8,128)S(1)} fusion(f32[32,128,128]{2,0,1:T(8,128)S(1)} %fusion.66, f32[32,128,128]{2,0,1:T(8,128)S(1)} %fusion.68), kind=kOutput, calls=%fused_computation.11.clone.1 | convolution fusion | flops 805306368 | bytes 6291456 | tf_op jit(solution)/shard_map/while/body/eval_jaxpr/ptu,puv->ptv/dot_general | solution.py:83
  81.8 6.1 %fusion.68 = f32[32,128,128]{2,0,1:T(8,128)S(1)} fusion(s32[32]{0:T(128)S(1)} %get-tuple-element.152, f32[8,8,128,128]{3,2,1,0:T(8,128)} %bitcast.92), kind=kOutput, calls=%fused_computation.2.clone.1 | convolution fusion | flops 402655232 | bytes 6291584 | tf_op jit(solution)/shard_map/while/body/eval_jaxpr/dot_general | solution.py:28
  87.9 5.0 %fusion.66 = f32[32,128,128]{2,0,1:T(8,128)S(1)} fusion(s32[32]{0:T(128)S(1)} %fusion.65, f32[6,8,128,128]{3,2,1,0:T(8,128)} %bitcast.89), kind=kOutput, calls=%fused_computation.6.clone.1 | convolution fusion | flops 301991424 | bytes 5243008 | tf_op jit(solution)/shard_map/while/body/eval_jaxpr/dot_general | solution.py:28
  100.3 6.1 %fusion.68 = f32[32,128,128]{2,0,1:T(8,128)S(1)} fusion(s32[32]{0:T(128)S(1)} %get-tuple-element.152, f32[8,8,128,128]{3,2,1,0:T(8,128)} %bitcast.92), kind=kOutput, calls=%fused_computation.2.clone.1 | convolution fusion | flops 402655232 | bytes 6291584 | tf_op jit(solution)/shard_map/while/body/eval_jaxpr/dot_general | solution.py:28
  106.3 5.0 %fusion.66 = f32[32,128,128]{2,0,1:T(8,128)S(1)} fusion(s32[32]{0:T(128)S(1)} %fusion.65, f32[6,8,128,128]{3,2,1,0:T(8,128)} %bitcast.89), kind=kOutput, calls=%fused_computation.6.clone.1 | convolution fusion | flops 301991424 | bytes 5243008 | tf_op jit(solution)/shard_map/while/body/eval_jaxpr/dot_general | solution.py:28
  111.4 4.6 %fusion.69 = f32[32,128,128]{2,1,0:T(8,128)S(1)} fusion(f32[32,128,128]{2,0,1:T(8,128)S(1)} %fusion.66, f32[32,128,128]{2,0,1:T(8,128)S(1)} %fusion.68), kind=kOutput, calls=%fused_computation.11.clone.1 | convolution fusion | flops 805306368 | bytes 6291456 | tf_op jit(solution)/shard_map/while/body/eval_jaxpr/ptu,puv->ptv/dot_general | solution.py:83
  118.8 6.1 %fusion.68 = f32[32,128,128]{2,0,1:T(8,128)S(1)} fusion(s32[32]{0:T(128)S(1)} %get-tuple-element.152, f32[8,8,128,128]{3,2,1,0:T(8,128)} %bitcast.92), kind=kOutput, calls=%fused_computation.2.clone.1 | convolution fusion | flops 402655232 | bytes 6291584 | tf_op jit(solution)/shard_map/while/body/eval_jaxpr/dot_general | solution.py:28
  124.8 5.0 %fusion.66 = f32[32,128,128]{2,0,1:T(8,128)S(1)} fusion(s32[32]{0:T(128)S(1)} %fusion.65, f32[6,8,128,128]{3,2,1,0:T(8,128)} %bitcast.89), kind=kOutput, calls=%fused_computation.6.clone.1 | convolution fusion | flops 301991424 | bytes 5243008 | tf_op jit(solution)/shard_map/while/body/eval_jaxpr/dot_general | solution.py:28
  137.2 6.1 %fusion.68 = f32[32,128,128]{2,0,1:T(8,128)S(1)} fusion(s32[32]{0:T(128)S(1)} %get-tuple-element.152, f32[8,8,128,128]{3,2,1,0:T(8,128)} %bitcast.92), kind=kOutput, calls=%fused_computation.2.clone.1 | convolution fusion | flops 402655232 | bytes 6291584 | tf_op jit(solution)/shard_map/while/body/eval_jaxpr/dot_general | solution.py:28
  143.3 5.0 %fusion.66 = f32[32,128,128]{2,0,1:T(8,128)S(1)} fusion(s32[32]{0:T(128)S(1)} %fusion.65, f32[6,8,128,128]{3,2,1,0:T(8,128)} %bitcast.89), kind=kOutput, calls=%fused_computation.6.clone.1 | convolution fusion | flops 301991424 | bytes 5243008 | tf_op jit(solution)/shard_map/while/body/eval_jaxpr/dot_general | solution.py:28
  148.3 4.6 %fusion.69 = f32[32,128,128]{2,1,0:T(8,128)S(1)} fusion(f32[32,128,128]{2,0,1:T(8,128)S(1)} %fusion.66, f32[32,128,128]{2,0,1:T(8,128)S(1)} %fusion.68), kind=kOutput, calls=%fused_computation.11.clone.1 | convolution fusion | flops 805306368 | bytes 6291456 | tf_op jit(solution)/shard_map/while/body/eval_jaxpr/ptu,puv->ptv/dot_general | solution.py:83
  155.7 6.1 %fusion.68 = f32[32,128,128]{2,0,1:T(8,128)S(1)} fusion(s32[32]{0:T(128)S(1)} %get-tuple-element.152, f32[8,8,128,128]{3,2,1,0:T(8,128)} %bitcast.92), kind=kOutput, calls=%fused_computation.2.clone.1 | convolution fusion | flops 402655232 | bytes 6291584 | tf_op jit(solution)/shard_map/while/body/eval_jaxpr/dot_general | solution.py:28
  161.8 5.0 %fusion.66 = f32[32,128,128]{2,0,1:T(8,128)S(1)} fusion(s32[32]{0:T(128)S(1)} %fusion.65, f32[6,8,128,128]{3,2,1,0:T(8,128)} %bitcast.89), kind=kOutput, calls=%fused_computation.6.clone.1 | convolution fusion | flops 301991424 | bytes 5243008 | tf_op jit(solution)/shard_map/while/body/eval_jaxpr/dot_general | solution.py:28
  174.2 6.1 %fusion.68 = f32[32,128,128]{2,0,1:T(8,128)S(1)} fusion(s32[32]{0:T(128)S(1)} %get-tuple-element.152, f32[8,8,128,128]{3,2,1,0:T(8,128)} %bitcast.92), kind=kOutput, calls=%fused_computation.2.clone.1 | convolution fusion | flops 402655232 | bytes 6291584 | tf_op jit(solution)/shard_map/while/body/eval_jaxpr/dot_general | solution.py:28
  180.3 5.0 %fusion.66 = f32[32,128,128]{2,0,1:T(8,128)S(1)} fusion(s32[32]{0:T(128)S(1)} %fusion.65, f32[6,8,128,128]{3,2,1,0:T(8,128)} %bitcast.89), kind=kOutput, calls=%fused_computation.6.clone.1 | convolution fusion | flops 301991424 | bytes 5243008 | tf_op jit(solution)/shard_map/while/body/eval_jaxpr/dot_general | solution.py:28
  192.7 6.1 %fusion.68 = f32[32,128,128]{2,0,1:T(8,128)S(1)} fusion(s32[32]{0:T(128)S(1)} %get-tuple-element.152, f32[8,8,128,128]{3,2,1,0:T(8,128)} %bitcast.92), kind=kOutput, calls=%fused_computation.2.clone.1 | convolution fusion | flops 402655232 | bytes 6291584 | tf_op jit(solution)/shard_map/while/body/eval_jaxpr/dot_general | solution.py:28
  198.7 5.0 %fusion.66 = f32[32,128,128]{2,0,1:T(8,128)S(1)} fusion(s32[32]{0:T(128)S(1)} %fusion.65, f32[6,8,128,128]{3,2,1,0:T(8,128)} %bitcast.89), kind=kOutput, calls=%fused_computation.6.clone.1 | convolution fusion | flops 301991424 | bytes 5243008 | tf_op jit(solution)/shard_map/while/body/eval_jaxpr/dot_general | solution.py:28
  211.1 53.5 %all_to_all.10 = f32[8,8,128,128]{3,1,2,0:T(8,128)} all-to-all(f32[8,8,128,128]{3,1,2,0:T(8,128)} %get-tuple-element.52), channel_id=1, replica_groups=mesh['rows'=8,'blk'=4] {'rows'}, dimensions={0} | all-to-all | bytes 8388608 | tf_op jit(solution)/shard_map/all_to_all | solution.py:90
  (83 shorter events, 73.4 us)
Async XLA Ops:
  0.0 1.1 copy-start
  0.0 3.2 %copy-start.1 = (f32[12,128,128]{2,1,0:T(8,128)S(1)}, f32[12,128,128]{2,1,0:T(8,128)}, u32[]{:S(2)}) copy-start(f32[12,128,128]{2,1,0:T(8,128)} %param.12) | copy-start | bytes 2359300
  1.1 9.7 %copy-start.3 = (s32[8,32]{1,0:T(8,128)S(1)}, s32[8,32]{1,0:T(8,128)}, u32[]{:S(2)}) copy-start(s32[8,32]{1,0:T(8,128)} %param.15) | copy-start | bytes 3076
  1.1 9.8 %copy-start.6 = (s32[8]{0:T(128)S(1)}, s32[8]{0:T(128)}, u32[]{:S(2)}) copy-start(s32[8]{0:T(128)} %param.17) | copy-start | bytes 100
  1.1 28.4 %copy-start.4 = (s32[8,32]{1,0:T(8,128)S(1)}, s32[8,32]{1,0:T(8,128)}, u32[]{:S(2)}) copy-start(s32[8,32]{1,0:T(8,128)} %param.16) | copy-start | bytes 3076
  1.1 28.5 %copy-start.5 = (s32[8,32]{1,0:T(8,128)S(1)}, s32[8,32]{1,0:T(8,128)}, u32[]{:S(2)}) copy-start(s32[8,32]{1,0:T(8,128)} %param.14) | copy-start | bytes 3076
  5.8 23.7 %collective-permute-start = (f32[12,128,128]{2,1,0:T(8,128)}, f32[12,128,128]{2,1,0:T(8,128)S(1)}, u32[]{:S(2)}, u32[]{:S(2)}) collective-permute-start(f32[12,128,128]{2,1,0:T(8,128)} %get-tuple-element.98), channel_id=1, source_target_pairs={{0,1},{1,2},{2,3},{3,0},{4,5},{5,6},{6,7},{7,4},{8,9},{9,10},{10,1... | collective-permute-start | bytes 2359304 | tf_op jit(solution)/shard_map/ppermute | solution.py:17
  8.9 36.3 %collective-permute-start.1 = (f32[12,128,128]{2,1,0:T(8,128)}, f32[12,128,128]{2,1,0:T(8,128)S(1)}, u32[]{:S(2)}, u32[]{:S(2)}) collective-permute-start(f32[12,128,128]{2,1,0:T(8,128)} %get-tuple-element.98), channel_id=1, source_target_pairs={{0,3},{1,0},{2,1},{3,2},{4,7},{5,4},{6,5},{7,6},{8,11},{9,8},{10,9... | collective-permute-start | bytes 2359304 | tf_op jit(solution)/shard_map/ppermute | solution.py:20
  29.5 32.9 %collective-permute-start.2 = (f32[12,128,128]{2,1,0:T(8,128)S(1)}, f32[12,128,128]{2,1,0:T(8,128)S(1)}, u32[]{:S(2)}, u32[]{:S(2)}) collective-permute-start(f32[12,128,128]{2,1,0:T(8,128)S(1)} %collective-permute-done), channel_id=1, source_target_pairs={{0,1},{1,2},{2,3},{3,0},{4,5},{5,6},{6,7},{7,4},{8,9},{9,10},{10,1... | collective-permute-start | bytes 2359304 | tf_op jit(solution)/shard_map/ppermute | solution.py:17
  31.0 8.6 %all-to-all-start = ((s32[8,1,128]{2,1,0:T(1,128)}), s32[8,1,128]{2,1,0:T(1,128)S(1)}, u32[]{:S(2)}, u32[]{:S(2)}) async-start(s32[8,1,128]{2,1,0:T(1,128)} %reshape.85), calls=%async_computation | async-start | bytes 8192 | tf_op jit(solution)/shard_map/all_to_all | solution.py:74
  264.7 2.5 copy-start.2
